TPU v7x, 256 devices: a whole 4x4x8 slice. The times are simulated.
256 devices in a mesh: grid: 64 (over z, y, core), lev: 4 (over x).
Axes of the slice: x: 4, y: 4, z: 8, core: 2. Of those that a mesh axis runs over, the one named last changes fastest.
Arguments:
- prior_fields: float32 [128, 8, 32768], P('grid', 'lev'), may hold values from -6 to 6
- channel_weights: float32 [8, 4], P('lev'), may hold values from 0.1 to 1
- obs_owner: int32 [4], replicated, may hold values from 0 to 63
- obs_offset: int32 [4, 4, 64], replicated, may hold values from 0 to 511
- obs_value: float32 [4, 4, 64], P(None, 'lev'), may hold values from -30 to 30
- obs_error: float32 [4, 4, 64], P(None, 'lev'), may hold values from 0.5 to 2
- ancestors: int32 [4, 4, 64, 128], P(None, 'lev', 'grid'), may hold values from 0 to 127
Outputs:
- posterior_fields: float32 [128, 8, 32768], P('grid', 'lev')
All inputs are finite; a program needn't handle non-finite values.
Results may differ from a plain program's by a relative error of at most 0.0003.
Values sent between devices are 32-bit elements; how exact they have to be, the bound alone decides.
A program may use at most 128 MiB of HBM per device.

v0:
```python
import jax
import jax.numpy as jnp
from jax import lax
from jax.sharding import PartitionSpec as P

NB = 4
HIGH = lax.Precision.HIGHEST


def spread(value, axis, source):
    kept = jnp.where(lax.axis_index(axis) == source, value, 0).astype(value.dtype)
    return lax.psum(kept, axis)


def blend_matrices(prior_obs, observed, obs_dev, centres, positions, scale, parents):
    count = observed.shape[0]
    members = prior_obs.shape[1]
    innovation = ((observed[:, None] - prior_obs) / obs_dev[:, None]) ** 2
    distance = (centres[:, None] - positions[None, :]) / scale
    taper = jnp.exp(-0.5 * distance * distance)
    log_weight = -0.5 / count * jnp.dot(taper, innovation, precision=HIGH)
    top_value = jnp.max(log_weight, axis=1, keepdims=True)
    expo_weight = jnp.exp(log_weight - top_value)
    weight = expo_weight / jnp.sum(expo_weight, axis=1, keepdims=True)
    alpha = 0.8 * (1.0 - jnp.exp(-jnp.sum(taper, axis=1) / count))
    onehot = (parents[:, :, None] == jnp.arange(members, dtype=jnp.int32)[None, None, :]).astype(
        jnp.float32
    )
    identity = jnp.eye(members, dtype=jnp.float32)
    remain = 1.0 - alpha
    return (
        alpha[:, None, None] * onehot
        + remain[:, None, None] * identity[None]
        + (weight - 1.0 / members)[:, None, :]
    )


def body(prior_fields, channel_weights, obs_owner, obs_offset, obs_value, obs_error, ancestors):
    grid_count = lax.axis_size("grid")
    member_slab, group_depth, cells = prior_fields.shape
    members = member_slab * grid_count
    block_cells = cells // grid_count
    local_regions = ancestors.shape[2]
    region_cells = block_cells // local_regions
    scale = local_regions * grid_count / 2.0
    groups = channel_weights.shape[1]
    count = obs_offset.shape[2]
    group = lax.axis_index("lev")
    block = lax.axis_index("grid")
    region_list = jnp.arange(local_regions, dtype=jnp.int32)
    centres = (block * local_regions + region_list).astype(jnp.float32) + 0.5
    first_cells = obs_offset[0].reshape(-1)
    fields = lax.all_to_all(prior_fields, "grid", split_axis=2, concat_axis=0, tiled=True)
    picked = fields[:, :, first_cells]
    for batch in range(NB):
        owner = obs_owner[batch]
        if batch > 0:
            picked = fields[:, :, obs_offset[batch].reshape(-1)]
        partial_value = jnp.einsum(
            "mlgk,lg->gkm",
            picked.reshape(members, group_depth, groups, count),
            channel_weights,
            precision=HIGH,
        )
        shared = spread(partial_value, "grid", owner)
        priors = lax.psum(shared, "lev")
        own_priors = lax.dynamic_index_in_dim(priors, group, 0, keepdims=False)
        own_offsets = lax.dynamic_index_in_dim(obs_offset[batch], group, 0, keepdims=False)
        positions = (owner * block_cells + own_offsets).astype(jnp.float32) / region_cells
        blend = blend_matrices(
            own_priors,
            obs_value[batch, 0],
            obs_error[batch, 0],
            centres,
            positions,
            scale,
            ancestors[batch, 0],
        )
        slab = fields.reshape(members, group_depth, local_regions, region_cells)
        mixed = jnp.einsum("rjm,mlrc->jlrc", blend, slab, precision=HIGH)
        fields = mixed.reshape(members, group_depth, block_cells)
    return lax.all_to_all(fields, "grid", split_axis=0, concat_axis=2, tiled=True)


def solution(mesh):
    in_specs = (
        P("grid", "lev", None),
        P("lev", None),
        P(),
        P(),
        P(None, "lev", None),
        P(None, "lev", None),
        P(None, "lev", "grid", None),
    )
    out_specs = P("grid", "lev", None)
    return jax.shard_map(body, mesh=mesh, in_specs=in_specs, out_specs=out_specs, check_vma=False)
```

profile of v0, /device:TPU:1, one launch (start us, length us, event | category | flops | bytes accessed | tf_op | source)
XLA Modules:
  0.0 1151.4 jit_solution(4428390036950253252)
XLA Ops:
  6.5 32.4 %copy.30 = f32[2,2,32768]{1,0,2:T(2,128)} copy(f32[2,2,32768]{2,1,0:T(2,128)} %param.7) | data formatting | bytes 1048576 | tf_op args[0]
  39.0 49.5 %reshape.797 = f32[64,1,2048]{2,1,0:T(1,128)} reshape(f32[32768,2,2]{2,1,0:T(2,128)} %bitcast.174) | data formatting | bytes 1048576
  88.5 13.2 %all-to-all-start = ((f32[64,1,2048]{2,1,0:T(1,128)}), f32[64,1,2048]{2,1,0:T(1,128)S(1)}, u32[]{:S(2)}, u32[]{:S(2)}) async-start(f32[64,1,2048]{2,1,0:T(1,128)} %reshape.797), calls=%async_computation | async-start | bytes 1048576 | tf_op jit(solution)/shard_map/all_to_all | solution.py:53
  101.8 0.1 reshape_squeeze.13
  101.9 0.1 reshape_squeeze.12
  101.9 0.7 fusion.106
  103.3 16.1 %all-to-all-done = f32[64,1,2048]{2,1,0:T(1,128)S(1)} async-done(((f32[64,1,2048]{2,1,0:T(1,128)}), f32[64,1,2048]{2,1,0:T(1,128)S(1)}, u32[]{:S(2)}, u32[]{:S(2)}) %all-to-all-start) | async-done | bytes 524320 | tf_op jit(solution)/shard_map/all_to_all | solution.py:53
  119.4 0.5 broadcast.610
  119.9 1.9 reduce.32
  121.8 53.4 %reshape.798 = f32[32768,2,2]{2,1,0:T(2,128)} reshape(f32[64,2048]{1,0:T(8,128)S(1)} %reduce.32) | data formatting | bytes 1048576
  175.2 35.6 %copy.31 = f32[2,2,64,512]{3,0,2,1:T(2,128)S(1)} copy(f32[2,2,64,512]{1,0,3,2:T(2,128)} %bitcast.173) | data formatting | bytes 1048576 | tf_op jit(solution)/shard_map/all_to_all | solution.py:53
  210.9 0.4 all_to_all.29
  211.2 0.2 copy.32
  211.5 1.0 gather_fusion
  212.5 0.1 multiply_reduce_fusion.3
  212.6 0.7 select_bitcast_fusion.3
  213.3 0.0 all-reduce.11.cloned.1.call-start
  214.0 169.1 %all-reduce.9.cloned.1.call-done = f32[4,64,128]{2,1,0:T(8,128)} async-done(((f32[4,64,128]{2,1,0:T(8,128)}), f32[4,64,128]{2,1,0:T(8,128)}) %all-reduce.9.cloned.1.call-update) | async-done | bytes 131088 | tf_op jit(solution)/shard_map/psum | solution.py:12
  383.2 0.6 fusion.104
  385.2 0.1 reshape_squeeze.15
  385.3 0.1 reshape_squeeze.14
  385.4 41.5 %all-reduce.11.cloned.1.call-done = f32[4,64,128]{2,1,0:T(8,128)} async-done(((f32[4,64,128]{2,1,0:T(8,128)}), f32[4,64,128]{2,1,0:T(8,128)}) %all-reduce.11.cloned.1.call-update) | async-done | bytes 131088 | tf_op jit(solution)/shard_map/psum | solution.py:66
  426.9 1.6 fusion.107
  428.4 1.3 fusion.97
  429.8 1.3 divide_add_fusion.3
  431.1 0.6 fusion.7
  431.8 0.2 copy.34
  432.0 1.0 gather_fusion.1
  433.0 0.1 multiply_reduce_fusion.2
  433.1 0.7 select_bitcast_fusion.2
  434.5 175.3 %all-reduce.13.cloned.1.call-done = f32[4,64,128]{2,1,0:T(8,128)} async-done(((f32[4,64,128]{2,1,0:T(8,128)}), f32[4,64,128]{2,1,0:T(8,128)}) %all-reduce.13.cloned.1.call-update) | async-done | bytes 131088 | tf_op jit(solution)/shard_map/psum | solution.py:12
  609.8 0.2 all-reduce.17.cloned.1.call-start
  610.1 0.6 fusion.103
  610.7 0.1 copy.66
  612.1 41.4 %all-reduce.15.cloned.1.call-done = f32[4,64,128]{2,1,0:T(8,128)} async-done(((f32[4,64,128]{2,1,0:T(8,128)}), f32[4,64,128]{2,1,0:T(8,128)}) %all-reduce.15.cloned.1.call-update) | async-done | bytes 131088 | tf_op jit(solution)/shard_map/psum | solution.py:66
  653.5 1.6 fusion.108
  655.1 1.3 fusion.98
  656.4 1.3 divide_add_fusion.2
  657.8 1.0 convolution_bitcast_fusion.2
  658.8 0.4 copy.37
  659.2 1.0 gather_fusion.2
  660.2 0.4 multiply_reduce_fusion.1
  660.6 0.7 select_bitcast_fusion.1
  662.0 175.4 %all-reduce.17.cloned.1.call-done = f32[4,64,128]{2,1,0:T(8,128)} async-done(((f32[4,64,128]{2,1,0:T(8,128)}), f32[4,64,128]{2,1,0:T(8,128)}) %all-reduce.17.cloned.1.call-update) | async-done | bytes 131088 | tf_op jit(solution)/shard_map/psum | solution.py:12
  837.4 0.6 fusion.102
  839.4 41.5 %all-reduce.19.cloned.1.call-done = f32[4,64,128]{2,1,0:T(8,128)} async-done(((f32[4,64,128]{2,1,0:T(8,128)}), f32[4,64,128]{2,1,0:T(8,128)}) %all-reduce.19.cloned.1.call-update) | async-done | bytes 131088 | tf_op jit(solution)/shard_map/psum | solution.py:66
  880.9 1.6 fusion.109
  882.5 1.3 fusion.99
  883.9 1.3 divide_add_fusion.1
  885.2 0.7 convolution_bitcast_fusion.1
  885.9 0.4 copy.38
  886.3 1.0 gather_fusion.3
  887.3 0.4 multiply_reduce_fusion
  887.7 0.7 select_bitcast_fusion
  888.4 176.1 %all-reduce.21.cloned.1.call-done = f32[4,64,128]{2,1,0:T(8,128)} async-done(((f32[4,64,128]{2,1,0:T(8,128)}), f32[4,64,128]{2,1,0:T(8,128)}) %all-reduce.21.cloned.1.call-update) | async-done | bytes 131088 | tf_op jit(solution)/shard_map/psum | solution.py:12
  1065.2 0.6 fusion.101
  1066.5 41.8 %all-reduce.23.cloned.1.call-done = f32[4,64,128]{2,1,0:T(8,128)} async-done(((f32[4,64,128]{2,1,0:T(8,128)}), f32[4,64,128]{2,1,0:T(8,128)}) %all-reduce.23.cloned.1.call-update) | async-done | bytes 131088 | tf_op jit(solution)/shard_map/psum | solution.py:66
  1108.3 1.6 fusion.110
  1109.9 1.3 fusion.100
  1111.2 1.3 divide_add_fusion
  1112.6 0.7 convolution_bitcast_fusion
  1113.2 0.2 copy.39
  1113.5 30.3 %all_to_all.36 = f32[128,2,512]{2,1,0:T(2,128)S(1)} all-to-all(f32[128,2,512]{2,1,0:T(2,128)S(1)} %copy.39), channel_id=1, replica_groups=mesh['grid'=64,'lev'=4] {'grid'}, dimensions={0} | all-to-all | bytes 1048576 | tf_op jit(solution)/shard_map/all_to_all | solution.py:82
  1143.7 0.8 copy.67
  (37 shorter events, 0.5 us)
Async XLA Ops:
  39.0 62.8 %copy-start.1 = (s32[4,4,64]{2,1,0:T(4,128)S(1)}, s32[4,4,64]{2,1,0:T(4,128)}, u32[]{:S(2)}) copy-start(s32[4,4,64]{2,1,0:T(4,128)} %param.10) | copy-start | bytes 12292
  39.0 63.0 %copy-start.2 = (s32[4]{0:T(128)S(1)}, s32[4]{0:T(128)}, u32[]{:S(2)}) copy-start(s32[4]{0:T(128)} %param.9) | copy-start | bytes 52
  39.0 64.3 %copy-start.4 = (f32[4,1,64]{2,1,0:T(1,128)S(1)}, f32[4,1,64]{2,1,0:T(1,128)}, u32[]{:S(2)}) copy-start(f32[4,1,64]{2,1,0:T(1,128)} %param.12) | copy-start | bytes 3076
  39.0 64.3 %copy-start.5 = (f32[4,1,64]{2,1,0:T(1,128)S(1)}, f32[4,1,64]{2,1,0:T(1,128)}, u32[]{:S(2)}) copy-start(f32[4,1,64]{2,1,0:T(1,128)} %param.11) | copy-start | bytes 3076
  88.5 30.9 %all-to-all-start = ((f32[64,1,2048]{2,1,0:T(1,128)}), f32[64,1,2048]{2,1,0:T(1,128)S(1)}, u32[]{:S(2)}, u32[]{:S(2)}) async-start(f32[64,1,2048]{2,1,0:T(1,128)} %reshape.797), calls=%async_computation | async-start | bytes 1048576 | tf_op jit(solution)/shard_map/all_to_all | solution.py:53
  101.7 281.4 %all-reduce.9.cloned.1.call-start = ((), (), s32[]{:S(2)}) async-start(), calls=%async_computation.2 | async-start | bytes 262144 | tf_op jit(solution)/shard_map/psum | solution.py:12
  175.2 37.3 %copy-start = (f32[2,4]{1,0:T(2,128)S(1)}, f32[2,4]{1,0:T(2,128)}, u32[]{:S(2)}) copy-start(f32[2,4]{1,0:T(2,128)} %param.8) | copy-start | bytes 100
  175.2 38.1 %copy-start.3 = (s32[4,1,1,128]{3,2,1,0:T(1,128)S(1)}, s32[4,1,1,128]{3,2,1,0:T(1,128)}, u32[]{:S(2)}) copy-start(s32[4,1,1,128]{3,2,1,0:T(1,128)} %param.13) | copy-start | bytes 6148
  213.3 213.6 %all-reduce.11.cloned.1.call-start = ((), (), s32[]{:S(2)}) async-start(), calls=%async_computation.3 | async-start | bytes 262144 | tf_op jit(solution)/shard_map/psum | solution.py:66
  383.1 226.7 %all-reduce.13.cloned.1.call-start = ((), (), s32[]{:S(2)}) async-start(), calls=%async_computation.4 | async-start | bytes 262144 | tf_op jit(solution)/shard_map/psum | solution.py:12
  433.8 219.7 %all-reduce.15.cloned.1.call-start = ((), (), s32[]{:S(2)}) async-start(), calls=%async_computation.5 | async-start | bytes 262144 | tf_op jit(solution)/shard_map/psum | solution.py:66
  609.8 227.5 %all-reduce.17.cloned.1.call-start = ((), (), s32[]{:S(2)}) async-start(), calls=%async_computation.6 | async-start | bytes 262144 | tf_op jit(solution)/shard_map/psum | solution.py:12
  661.3 219.6 %all-reduce.19.cloned.1.call-start = ((), (), s32[]{:S(2)}) async-start(), calls=%async_computation.7 | async-start | bytes 262144 | tf_op jit(solution)/shard_map/psum | solution.py:66
  837.4 227.1 %all-reduce.21.cloned.1.call-start = ((), (), s32[]{:S(2)}) async-start(), calls=%async_computation.8 | async-start | bytes 262144 | tf_op jit(solution)/shard_map/psum | solution.py:12
  888.3 220.0 %all-reduce.23.cloned.1.call-start = ((), (), s32[]{:S(2)}) async-start(), calls=%async_computation.9 | async-start | bytes 262144 | tf_op jit(solution)/shard_map/psum | solution.py:66
Sparse Core Ops, SparseCore 0:
  213.4 169.6 all-reduce.8
  385.4 41.3 all-reduce.10
  433.9 175.8 all-reduce.12
  612.1 41.3 all-reduce.14
  661.4 175.8 all-reduce.16
  839.5 41.3 all-reduce.18
  888.5 175.9 all-reduce.20
  1066.9 41.3 all-reduce.22
where the time goes:
time: 1160 us; the launch traced here: 1150 us
  waiting for transfers between devices  878 us (76%)
  local copies, waits for them, and re-layouts  179 us (15%)
  blocking collectives  30.3 us (3%)
  between operations  21.8 us (2%)
  other arithmetic  18.7 us (2%)
  starting transfers between devices  13.7 us (1%)
    psum x4, waiting for transfers between devices, spread(): return lax.psum(kept, axis)  696 us
    psum x4, waiting for transfers between devices, body(): priors = lax.psum(shared, 'lev')  166 us
    unnamed x18, local copies, waits for them, and re-layouts  136 us
    all_to_all x4, local copies, waits for them, and re-layouts, body(): lax.all_to_all(prior_fields, 'grid', split_axis=2, concat_axis=0, tiled=T...  36.7 us
    all_to_all x1, blocking collectives, body(): lax.all_to_all(fields, 'grid', split_axis=0, concat_axis=2, tiled=True)  30.3 us
  transfers between devices with their start and end apart: 9, of which 9 were waited for; matrix products, arithmetic and copies ran while one was open for 0% of the time, Pallas kernels for 0%

commit v1 on v0

--- a/solution.py
+++ b/solution.py
@@ -50,7 +50,12 @@
     region_list = jnp.arange(local_regions, dtype=jnp.int32)
     centres = (block * local_regions + region_list).astype(jnp.float32) + 0.5
     first_cells = obs_offset[0].reshape(-1)
-    fields = lax.all_to_all(prior_fields, "grid", split_axis=2, concat_axis=0, tiled=True)
+    fields = jnp.concatenate(
+        lax.all_to_all(
+            jnp.stack(jnp.split(prior_fields, lax.axis_size("grid"), axis=2)), "grid", 0, 0
+        ),
+        axis=0,
+    )
     picked = fields[:, :, first_cells]
     for batch in range(NB):
         owner = obs_owner[batch]

time: 1160 us -> 1070 us (0.922)
  local copies, waits for them, and re-layouts: 179 us -> 90.7 us
    unnamed x18 -> x76, local copies, waits for them, and re-layouts: 136 us -> 81.8 us
    all_to_all x4 -> x0, local copies, waits for them, and re-layouts: 36.7 us -> none  [body(): lax.all_to_all(prior_fields, 'grid', split_axis=2, concat_axis=0, tiled=T...]
where the time goes in v1:
time: 1070 us; the launch traced here: 1060 us
  waiting for transfers between devices  879 us (82%)
  local copies, waits for them, and re-layouts  90.7 us (8%)
  blocking collectives  30.3 us (3%)
  between operations  21.3 us (2%)
  other arithmetic  17.4 us (2%)
  starting transfers between devices  13.6 us (1%)
    psum x4, waiting for transfers between devices, spread(): return lax.psum(kept, axis)  696 us
    psum x4, waiting for transfers between devices, body(): priors = lax.psum(shared, 'lev')  167 us
    unnamed x76, local copies, waits for them, and re-layouts  81.8 us
    all_to_all x1, blocking collectives, body(): lax.all_to_all(fields, 'grid', split_axis=0, concat_axis=2, tiled=True)  30.3 us
  transfers between devices with their start and end apart: 9, of which 9 were waited for; matrix products, arithmetic and copies ran while one was open for 0% of the time, Pallas kernels for 0%

profile of v1, /device:TPU:1, one launch (start us, length us, event | category | flops | bytes accessed | tf_op | source)
XLA Modules:
  0.0 1061.7 jit_solution(10447274248523467401)
XLA Ops:
  6.5 1.3 constant_dynamic-update-slice_fusion.63
  7.8 1.3 constant_dynamic-update-slice_fusion.62
  10.4 1.3 constant_dynamic-update-slice_fusion.60
  11.7 1.3 constant_dynamic-update-slice_fusion.59
  13.0 1.3 constant_dynamic-update-slice_fusion.58
  14.3 1.3 constant_dynamic-update-slice_fusion.57
  15.6 1.3 constant_dynamic-update-slice_fusion.56
  16.9 1.3 constant_dynamic-update-slice_fusion.55
  19.5 1.3 constant_dynamic-update-slice_fusion.53
  20.8 1.3 constant_dynamic-update-slice_fusion.52
  23.4 1.3 constant_dynamic-update-slice_fusion.50
  24.7 1.3 constant_dynamic-update-slice_fusion.49
  26.0 1.3 constant_dynamic-update-slice_fusion.48
  27.3 1.3 constant_dynamic-update-slice_fusion.47
  28.6 1.3 constant_dynamic-update-slice_fusion.46
  31.1 1.3 constant_dynamic-update-slice_fusion.44
  32.4 1.3 constant_dynamic-update-slice_fusion.43
  33.7 1.3 constant_dynamic-update-slice_fusion.42
  35.0 1.3 constant_dynamic-update-slice_fusion.41
  36.3 1.3 constant_dynamic-update-slice_fusion.40
  37.6 1.3 constant_dynamic-update-slice_fusion.39
  38.9 1.3 constant_dynamic-update-slice_fusion.38
  40.2 1.3 constant_dynamic-update-slice_fusion.37
  41.5 1.3 constant_dynamic-update-slice_fusion.36
  42.8 1.3 constant_dynamic-update-slice_fusion.35
  44.1 1.3 constant_dynamic-update-slice_fusion.34
  45.4 1.3 constant_dynamic-update-slice_fusion.33
  46.7 1.3 constant_dynamic-update-slice_fusion.32
  48.0 1.3 constant_dynamic-update-slice_fusion.31
  49.3 1.3 constant_dynamic-update-slice_fusion.30
  50.6 1.3 constant_dynamic-update-slice_fusion.29
  53.2 1.3 constant_dynamic-update-slice_fusion.27
  54.5 1.3 constant_dynamic-update-slice_fusion.26
  55.8 1.3 constant_dynamic-update-slice_fusion.25
  57.1 1.3 constant_dynamic-update-slice_fusion.24
  58.4 1.3 constant_dynamic-update-slice_fusion.23
  61.0 1.3 constant_dynamic-update-slice_fusion.21
  62.3 1.3 constant_dynamic-update-slice_fusion.20
  63.6 1.3 constant_dynamic-update-slice_fusion.19
  64.9 1.3 constant_dynamic-update-slice_fusion.18
  83.0 1.3 constant_dynamic-update-slice_fusion.4
  89.5 13.3 %all-to-all-start = ((f32[64,2,2,512]{3,2,1,0:T(2,128)}), f32[64,2,2,512]{3,2,1,0:T(2,128)S(1)}, u32[]{:S(2)}, u32[]{:S(2)}) async-start(f32[64,2,2,512]{3,2,1,0:T(2,128)} %constant_dynamic-update-slice_fusion), calls=%async_computation | async-start | bytes 1048576 | tf_op jit(solution)/shard_map/all_to_all | solution.py:54
  104.5 16.1 %all-to-all-done = f32[64,2,2,512]{3,2,1,0:T(2,128)S(1)} async-done(((f32[64,2,2,512]{3,2,1,0:T(2,128)}), f32[64,2,2,512]{3,2,1,0:T(2,128)S(1)}, u32[]{:S(2)}, u32[]{:S(2)}) %all-to-all-start) | async-done | bytes 524320 | tf_op jit(solution)/shard_map/all_to_all | solution.py:54
  123.7 169.2 %all-reduce.9.cloned.1.call-done = f32[4,64,128]{2,1,0:T(8,128)} async-done(((f32[4,64,128]{2,1,0:T(8,128)}), f32[4,64,128]{2,1,0:T(8,128)}) %all-reduce.9.cloned.1.call-update) | async-done | bytes 131088 | tf_op jit(solution)/shard_map/psum | solution.py:12
  295.0 41.6 %all-reduce.11.cloned.1.call-done = f32[4,64,128]{2,1,0:T(8,128)} async-done(((f32[4,64,128]{2,1,0:T(8,128)}), f32[4,64,128]{2,1,0:T(8,128)}) %all-reduce.11.cloned.1.call-update) | async-done | bytes 131088 | tf_op jit(solution)/shard_map/psum | solution.py:71
  336.6 1.6 fusion.107
  338.2 1.3 fusion.97
  339.6 1.3 divide_add_fusion.3
  345.0 175.4 %all-reduce.13.cloned.1.call-done = f32[4,64,128]{2,1,0:T(8,128)} async-done(((f32[4,64,128]{2,1,0:T(8,128)}), f32[4,64,128]{2,1,0:T(8,128)}) %all-reduce.13.cloned.1.call-update) | async-done | bytes 131088 | tf_op jit(solution)/shard_map/psum | solution.py:12
  522.5 41.7 %all-reduce.15.cloned.1.call-done = f32[4,64,128]{2,1,0:T(8,128)} async-done(((f32[4,64,128]{2,1,0:T(8,128)}), f32[4,64,128]{2,1,0:T(8,128)}) %all-reduce.15.cloned.1.call-update) | async-done | bytes 131088 | tf_op jit(solution)/shard_map/psum | solution.py:71
  564.2 1.6 fusion.108
  565.8 1.3 fusion.98
  567.1 1.3 divide_add_fusion.2
  572.3 175.4 %all-reduce.17.cloned.1.call-done = f32[4,64,128]{2,1,0:T(8,128)} async-done(((f32[4,64,128]{2,1,0:T(8,128)}), f32[4,64,128]{2,1,0:T(8,128)}) %all-reduce.17.cloned.1.call-update) | async-done | bytes 131088 | tf_op jit(solution)/shard_map/psum | solution.py:12
  749.7 41.6 %all-reduce.19.cloned.1.call-done = f32[4,64,128]{2,1,0:T(8,128)} async-done(((f32[4,64,128]{2,1,0:T(8,128)}), f32[4,64,128]{2,1,0:T(8,128)}) %all-reduce.19.cloned.1.call-update) | async-done | bytes 131088 | tf_op jit(solution)/shard_map/psum | solution.py:71
  791.3 1.6 fusion.109
  792.8 1.3 fusion.99
  794.2 1.3 divide_add_fusion.1
  798.7 176.0 %all-reduce.21.cloned.1.call-done = f32[4,64,128]{2,1,0:T(8,128)} async-done(((f32[4,64,128]{2,1,0:T(8,128)}), f32[4,64,128]{2,1,0:T(8,128)}) %all-reduce.21.cloned.1.call-update) | async-done | bytes 131088 | tf_op jit(solution)/shard_map/psum | solution.py:12
  976.7 41.9 %all-reduce.23.cloned.1.call-done = f32[4,64,128]{2,1,0:T(8,128)} async-done(((f32[4,64,128]{2,1,0:T(8,128)}), f32[4,64,128]{2,1,0:T(8,128)}) %all-reduce.23.cloned.1.call-update) | async-done | bytes 131088 | tf_op jit(solution)/shard_map/psum | solution.py:71
  1018.5 1.6 fusion.110
  1020.1 1.3 fusion.100
  1021.5 1.3 divide_add_fusion
  1023.7 30.3 %all_to_all.23 = f32[128,2,512]{2,1,0:T(2,128)S(1)} all-to-all(f32[128,2,512]{2,1,0:T(2,128)S(1)} %copy.28), channel_id=1, replica_groups=mesh['grid'=64,'lev'=4] {'grid'}, dimensions={0} | all-to-all | bytes 1048576 | tf_op jit(solution)/shard_map/all_to_all | solution.py:87
  (92 shorter events, 47.7 us)
Async XLA Ops:
  89.5 13.4 %copy-start = (s32[4,4,64]{2,1,0:T(4,128)S(1)}, s32[4,4,64]{2,1,0:T(4,128)}, u32[]{:S(2)}) copy-start(s32[4,4,64]{2,1,0:T(4,128)} %param.10) | copy-start | bytes 12292
  89.5 13.6 %copy-start.5 = (f32[2,4]{1,0:T(2,128)S(1)}, f32[2,4]{1,0:T(2,128)}, u32[]{:S(2)}) copy-start(f32[2,4]{1,0:T(2,128)} %param.8) | copy-start | bytes 100
  89.5 13.7 %copy-start.1 = (s32[4]{0:T(128)S(1)}, s32[4]{0:T(128)}, u32[]{:S(2)}) copy-start(s32[4]{0:T(128)} %param.9) | copy-start | bytes 52
  89.5 14.9 %copy-start.3 = (f32[4,1,64]{2,1,0:T(1,128)S(1)}, f32[4,1,64]{2,1,0:T(1,128)}, u32[]{:S(2)}) copy-start(f32[4,1,64]{2,1,0:T(1,128)} %param.12) | copy-start | bytes 3076
  89.5 14.9 %copy-start.4 = (f32[4,1,64]{2,1,0:T(1,128)S(1)}, f32[4,1,64]{2,1,0:T(1,128)}, u32[]{:S(2)}) copy-start(f32[4,1,64]{2,1,0:T(1,128)} %param.11) | copy-start | bytes 3076
  89.5 31.0 %all-to-all-start = ((f32[64,2,2,512]{3,2,1,0:T(2,128)}), f32[64,2,2,512]{3,2,1,0:T(2,128)S(1)}, u32[]{:S(2)}, u32[]{:S(2)}) async-start(f32[64,2,2,512]{3,2,1,0:T(2,128)} %constant_dynamic-update-slice_fusion), calls=%async_computation | async-start | bytes 1048576 | tf_op jit(solution)/shard_map/all_to_all | solution.py:54
  102.8 190.1 %all-reduce.9.cloned.1.call-start = ((), (), s32[]{:S(2)}) async-start(), calls=%async_computation.2 | async-start | bytes 262144 | tf_op jit(solution)/shard_map/psum | solution.py:12
  122.0 1.2 copy-start.2
  123.1 213.6 %all-reduce.11.cloned.1.call-start = ((), (), s32[]{:S(2)}) async-start(), calls=%async_computation.3 | async-start | bytes 262144 | tf_op jit(solution)/shard_map/psum | solution.py:71
  292.9 227.5 %all-reduce.13.cloned.1.call-start = ((), (), s32[]{:S(2)}) async-start(), calls=%async_computation.4 | async-start | bytes 262144 | tf_op jit(solution)/shard_map/psum | solution.py:12
  344.4 219.7 %all-reduce.15.cloned.1.call-start = ((), (), s32[]{:S(2)}) async-start(), calls=%async_computation.5 | async-start | bytes 262144 | tf_op jit(solution)/shard_map/psum | solution.py:71
  520.5 227.2 %all-reduce.17.cloned.1.call-start = ((), (), s32[]{:S(2)}) async-start(), calls=%async_computation.6 | async-start | bytes 262144 | tf_op jit(solution)/shard_map/psum | solution.py:12
  571.6 219.7 %all-reduce.19.cloned.1.call-start = ((), (), s32[]{:S(2)}) async-start(), calls=%async_computation.7 | async-start | bytes 262144 | tf_op jit(solution)/shard_map/psum | solution.py:71
  747.7 227.0 %all-reduce.21.cloned.1.call-start = ((), (), s32[]{:S(2)}) async-start(), calls=%async_computation.8 | async-start | bytes 262144 | tf_op jit(solution)/shard_map/psum | solution.py:12
  798.7 219.9 %all-reduce.23.cloned.1.call-start = ((), (), s32[]{:S(2)}) async-start(), calls=%async_computation.9 | async-start | bytes 262144 | tf_op jit(solution)/shard_map/psum | solution.py:71
Sparse Core Ops, SparseCore 0:
  123.2 169.6 all-reduce.8
  295.2 41.3 all-reduce.10
  344.6 175.8 all-reduce.12
  522.7 41.3 all-reduce.14
  571.7 175.9 all-reduce.16
  749.8 41.3 all-reduce.18
  798.8 175.8 all-reduce.20
  977.1 41.3 all-reduce.22
